TPU v7x, 128 devices: a whole 4x4x4 slice. The times are simulated.
128 devices in a mesh: rng: 8 (over z, y_hi), az: 16 (over y_lo, x, core).
Axes of the slice: x: 4, y: 4 (y_hi: 2, y_lo: 2; y = y_hi * 2 + y_lo), z: 4, core: 2. Of those that a mesh axis runs over, the one named last changes fastest.
Arguments:
- raw_swath: bfloat16 [8192, 2, 16384], P('rng', None, 'az'), may hold values from -6 to 6
- azimuth_filter: bfloat16 [8192, 2, 16384], P(('rng', 'az')), may hold values from -4 to 4
- anchors: int32 [8, 63, 2], replicated, may hold values from 0 to 15872, as said below
- owners: int32 [8, 63], replicated, may hold values from 0 to 15, as said below
- look_bands: int32 [8, 63, 3], replicated, may hold values from 0 to 384
Outputs:
- cross_spectra: float32 [8, 64, 2, 512, 128], P('rng', 'az')
Inputs may be any that keep to these rules, and one draw needn't show every extreme that they name: anchors[r, i] is the first line and the first column (in units of 64 cells) of imagette i in strip r; the column is below 16, and below 9 in the last strip; some imagette of each strip starts at line 16384 - 512. `owners`: in each strip every owner appears at most 4 times, and all but one owner exactly 4 times.
All inputs are finite; a program needn't handle non-finite values.
Results may differ from a plain program's by a relative error of at most 0.004.
Values may be sent and summed in bfloat16 or wider, within the bound.
No kernel may reach another device: no remote copies, remote signals or barrier semaphores. Data moves between devices by JAX's collectives and lax.ppermute only.
A program may use at most 128 MiB of HBM per device.

v0:
```python
import math

import jax
import jax.numpy as jnp
from jax import lax
from jax.sharding import PartitionSpec as P

AZ_OUTER = 128
AZ_INNER = 128
IMG_C = 512
IMG_L = 512
LOOK = 128
IMG_DEV = 4


full_turn = 2.0 * math.pi
epsilon = 1e-06


def passed_along(value, axis, steps):
    count = lax.axis_size(axis)
    first, last = (max(0, -steps), min(count, count - steps))
    return lax.ppermute(value, axis, [(source, source + steps) for source in range(first, last)])


def dft_table(length, sign):
    steps = jnp.arange(length, dtype=jnp.int32)
    phase = steps[:, None] * steps[None, :] % length
    angle = full_turn * phase.astype(jnp.float32) / length
    scale = 1.0 / math.sqrt(length)
    return (
        (jnp.cos(angle) * scale).astype(jnp.bfloat16),
        (sign * jnp.sin(angle) * scale).astype(jnp.bfloat16),
    )


def twiddle_table(sign):
    outer = jnp.arange(AZ_OUTER, dtype=jnp.int32)
    inner = jnp.arange(AZ_INNER, dtype=jnp.int32)
    phase = outer[:, None] * inner[None, :] % (AZ_OUTER * AZ_INNER)
    angle = full_turn * phase.astype(jnp.float32) / (AZ_OUTER * AZ_INNER)
    return (jnp.cos(angle), sign * jnp.sin(angle))


def mix(form, left, right):
    return jnp.einsum(form, left, right, preferred_element_type=jnp.float32)


def complex_sum(form, left_re, left_im, right_re, right_im):
    out_re = mix(form, left_re, right_re) - mix(form, left_im, right_im)
    out_im = mix(form, left_re, right_im) + mix(form, left_im, right_re)
    return (out_re, out_im)


def focus_turned(turned, response):
    sources = turned.shape[0]
    count = turned.shape[1]
    part_outer = AZ_OUTER // sources
    lines_re = turned[:, :, 0].reshape(sources, count, part_outer, AZ_INNER)
    lines_im = turned[:, :, 1].reshape(sources, count, part_outer, AZ_INNER)
    outer_re, outer_im = dft_table(AZ_OUTER, -1.0)
    outer_re = outer_re.reshape(sources, part_outer, AZ_OUTER)
    outer_im = outer_im.reshape(sources, part_outer, AZ_OUTER)
    inner_re, inner_im = dft_table(AZ_INNER, -1.0)
    twist_re, twist_im = twiddle_table(-1.0)
    first_re, first_im = complex_sum("scab,sak->ckb", lines_re, lines_im, outer_re, outer_im)
    section_re = (first_re * twist_re - first_im * twist_im).astype(jnp.bfloat16)
    section_im = (first_re * twist_im + first_im * twist_re).astype(jnp.bfloat16)
    second_re, second_im = complex_sum("ckb,bm->ckm", section_re, section_im, inner_re, inner_im)
    gain_re = response[:, 0].reshape(count, AZ_OUTER, AZ_INNER).astype(jnp.float32)
    gain_im = response[:, 1].reshape(count, AZ_OUTER, AZ_INNER).astype(jnp.float32)
    shaped_re = (second_re * gain_re - second_im * gain_im).astype(jnp.bfloat16)
    shaped_im = (second_re * gain_im + second_im * gain_re).astype(jnp.bfloat16)
    back_outer_re, back_outer_im = dft_table(AZ_OUTER, 1.0)
    back_inner_re, back_inner_im = dft_table(AZ_INNER, 1.0)
    untwist_re, untwist_im = twiddle_table(1.0)
    third_re, third_im = complex_sum(
        "ckm,mb->ckb", shaped_re, shaped_im, back_inner_re, back_inner_im
    )
    rest_re = (third_re * untwist_re - third_im * untwist_im).astype(jnp.bfloat16)
    rest_im = (third_re * untwist_im + third_im * untwist_re).astype(jnp.bfloat16)
    final_re, final_im = complex_sum("ckb,ka->cab", rest_re, rest_im, back_outer_re, back_outer_im)
    return jnp.stack([final_re.reshape(count, -1), final_im.reshape(count, -1)], axis=1).astype(
        jnp.bfloat16
    )


def azimuth_spectrum(image):
    table_re, table_im = dft_table(IMG_L, -1.0)
    out_re, out_im = complex_sum(
        "...cn,nf->...cf", image[..., 0, :], image[..., 1, :], table_re, table_im
    )
    return jnp.stack([out_re, out_im], axis=-2).astype(jnp.bfloat16)


def look_powers(spectrum, starts):
    back_re, back_im = dft_table(LOOK, 1.0)
    powers = []
    for number in range(3):
        band = lax.dynamic_slice_in_dim(spectrum, starts[number], LOOK, 2)
        look_re, look_im = complex_sum("cf,fm->cm", band[:, 0], band[:, 1], back_re, back_im)
        powers.append(look_re * look_re + look_im * look_im)
    return jnp.stack(powers, axis=1)


def from_powers(powers):
    ahead_re, ahead_im = dft_table(LOOK, -1.0)
    across_re_tab, across_im_tab = dft_table(IMG_C, -1.0)
    waves = []
    for number in range(3):
        power = powers[:, number]
        contrast = (power / (jnp.mean(power) + epsilon) - 1.0).astype(jnp.bfloat16)
        across_re = mix("pc,cm->pm", across_re_tab, contrast).astype(jnp.bfloat16)
        across_im = mix("pc,cm->pm", across_im_tab, contrast).astype(jnp.bfloat16)
        waves.append(complex_sum("pm,mv->pv", across_re, across_im, ahead_re, ahead_im))
    total_re = jnp.zeros((IMG_C, LOOK), jnp.float32)
    total_im = jnp.zeros((IMG_C, LOOK), jnp.float32)
    for first, second in ((0, 1), (1, 2), (0, 2)):
        one_re, one_im = waves[first]
        two_re, two_im = waves[second]
        total_re = total_re + one_re * two_re + one_im * two_im
        total_im = total_im + one_im * two_re - one_re * two_im
    return jnp.stack([total_re, total_im])


def cross_spectrum(spectrum, starts):
    return from_powers(look_powers(spectrum, starts))


def slot_table(owner_row, azimuth_count, capacity):
    labels = jnp.arange(azimuth_count, dtype=jnp.int32)
    owners_hot = (owner_row[:, None] == labels[None, :]).astype(jnp.int32)
    earlier = jnp.cumsum(owners_hot, axis=0) - owners_hot
    rank = jnp.sum(earlier * owners_hot, axis=1)
    match = (owner_row[None, None, :] == labels[:, None, None]) & (
        rank[None, None, :] == jnp.arange(capacity, dtype=jnp.int32)[None, :, None]
    )
    filled = jnp.any(match, axis=2)
    items = jnp.arange(owner_row.shape[0], dtype=jnp.int32)
    chosen = jnp.sum(jnp.where(match, items[None, None, :], 0), axis=2)
    return (filled, chosen)


def assemble(arrived, selector):
    total_rows = arrived.shape[0] * arrived.shape[1]
    flat = arrived.reshape(total_rows, -1)
    picked = jnp.dot(
        selector.astype(jnp.bfloat16), flat, preferred_element_type=jnp.float32
    ).astype(jnp.bfloat16)
    return picked


def shards(raw_swath, azimuth_filter, anchors, owners, look_bands):
    azimuth_count = lax.axis_size("az")
    strip = lax.axis_index("rng")
    column = lax.axis_index("az")
    pieces = raw_swath.reshape(
        azimuth_count, raw_swath.shape[0] // azimuth_count, 2, raw_swath.shape[2]
    )
    turned = lax.all_to_all(pieces, "az", split_axis=0, concat_axis=0, tiled=True)
    focused = focus_turned(turned, azimuth_filter)
    beyond = passed_along(focused, "rng", -1)
    width = focused.shape[0]
    span = IMG_C // width
    strip_anchors = lax.dynamic_index_in_dim(anchors, strip, 0, keepdims=False)
    strip_owners = lax.dynamic_index_in_dim(owners, strip, 0, keepdims=False)
    strip_bands = lax.dynamic_index_in_dim(look_bands, strip, 0, keepdims=False)
    filled, chosen = slot_table(strip_owners, azimuth_count, IMG_DEV)
    start_lines = strip_anchors[chosen, 0]
    start_columns = strip_anchors[chosen, 1]
    shifted = column + azimuth_count
    from_own = (start_columns <= column) & (column < start_columns + span)
    from_next = (start_columns <= shifted) & (shifted < start_columns + span)
    wanted = filled & (from_own | from_next)

    def cut_block(take_next, keep, first_line):
        own_part = lax.dynamic_slice_in_dim(focused, first_line, IMG_L, 2)
        next_part = lax.dynamic_slice_in_dim(beyond, first_line, IMG_L, 2)
        chosen_part = jnp.where(take_next, next_part, own_part)
        return jnp.where(keep, chosen_part, jnp.zeros_like(chosen_part))

    blocks = jax.vmap(jax.vmap(cut_block))(from_next, wanted, start_lines)
    mine = lax.dynamic_index_in_dim(chosen, column, 0, keepdims=False)
    mine_filled = lax.dynamic_index_in_dim(filled, column, 0, keepdims=False)
    mine_columns = strip_anchors[mine, 1]
    picks = (mine_columns[:, None] + jnp.arange(span, dtype=jnp.int32)[None, :]) % azimuth_count
    slot_index = jnp.arange(IMG_DEV, dtype=jnp.int32)[:, None]
    wanted_rows = (picks * IMG_DEV + slot_index).reshape(-1)
    selector = wanted_rows[:, None] == jnp.arange(azimuth_count * IMG_DEV, dtype=jnp.int32)[None, :]
    sent_spectra = azimuth_spectrum(blocks)
    arrived = lax.all_to_all(sent_spectra, "az", split_axis=0, concat_axis=0, tiled=True)
    images = assemble(arrived, selector).reshape(IMG_DEV, IMG_C, 2, IMG_L)
    results = jax.vmap(cross_spectrum)(images, strip_bands[mine])
    results = jnp.where(mine_filled[:, None, None, None], results, jnp.zeros_like(results))
    return results[None]


def solution(mesh):
    in_specs = (P("rng", None, "az"), P(("rng", "az"), None, None), P(), P(), P())
    out_specs = P("rng", "az", None, None, None)
    return jax.shard_map(shards, mesh=mesh, in_specs=in_specs, out_specs=out_specs, check_vma=False)
```

profile of v0, /device:TPU:50, one launch (start us, length us, event | category | flops | bytes accessed | tf_op | source)
XLA Modules:
  0.0 690.8 jit_solution(15067754803991692731)
XLA Ops:
  5.5 5.6 all-to-all-start
  11.7 11.2 %slice_convert_fusion.1 = (f32[64,1,16384]{2,1,0:T(1,128)}, f32[64,1,16384]{2,1,0:T(1,128)}) fusion(bf16[64,2,16384]{2,1,0:T(2,128)(2,1)} %param.6), kind=kLoop, calls=%fused_computation.28 | loop fusion | flops 2097152 | bytes 12582912 | tf_op jit(solution)/shard_map/convert_element_type | solution.py:70
  22.8 45.1 %all-to-all-done = bf16[16,64,2,1024]{3,1,2,0:T(8,128)(2,1)} async-done(((bf16[16,64,2,1024]{3,1,2,0:T(8,128)(2,1)}), bf16[16,64,2,1024]{3,1,2,0:T(8,128)(2,1)}, u32[]{:S(2)}, u32[]{:S(2)}) %all-to-all-start) | async-done | bytes 4194336 | tf_op jit(solution)/shard_map/all_to_all | solution.py:160
  113.2 17.3 %copy.159 = bf16[64,1,16384]{0,1,2:T(2,128)(2,1)} copy(bf16[64,1,16384]{2,0,1:T(8,128)(2,1)} %stack_reshape.8) | data formatting | bytes 4194304 | tf_op jit(solution)/shard_map/stack;reshape | solution.py:83
  130.5 12.8 %copy.160 = bf16[64,1,16384]{0,1,2:T(2,128)(2,1)} copy(bf16[64,1,16384]{2,0,1:T(8,128)(2,1)S(1)} %copy-done.3) | data formatting | bytes 4194304 | tf_op jit(solution)/shard_map/stack;reshape | solution.py:83
  143.3 24.7 %pad_maximum_fusion = bf16[64,2,16384]{0,1,2:T(2,128)(2,1)} fusion(bf16[64,1,16384]{0,1,2:T(2,128)(2,1)} %copy.160, bf16[64,1,16384]{0,1,2:T(2,128)(2,1)} %copy.159), kind=kLoop, calls=%fused_computation.10 | loop fusion | flops 8388608 | bytes 8388608 | tf_op jit(solution)/shard_map/stack | solution.py:83
  168.0 17.5 %copy.161 = bf16[64,2,16384]{2,0,1:T(8,128)(2,1)} copy(bf16[64,2,16384]{0,1,2:T(2,128)(2,1)} %pad_maximum_fusion) | data formatting | bytes 8388608 | tf_op jit(solution)/shard_map/stack | solution.py:83
  193.3 39.0 %gather_fusion.4 = bf16[64,64,2,512]{1,2,3,0:T(2,128)(2,1)} fusion(bf16[64,2,16384]{0,1,2:T(2,128)(2,1)} %pad_maximum_fusion, s32[64]{0:T(128)S(1)} %reshape.255), kind=kCustom, calls=%fused_computation.4 | custom fusion | bytes 16777984 | tf_op jit(solution)/shard_map/vmap(vmap())/gather | solution.py:177
  232.3 33.8 %copy.169 = bf16[64,64,2,512]{3,1,0,2:T(8,128)(2,1)} copy(bf16[64,64,2,512]{1,2,3,0:T(2,128)(2,1)} %gather_fusion.4) | data formatting | bytes 16777216 | tf_op jit(solution)/shard_map/vmap(vmap())/gather | solution.py:177
  266.1 16.4 %collective-permute-done = bf16[64,2,16384]{2,0,1:T(8,128)(2,1)} collective-permute-done((bf16[64,2,16384]{2,0,1:T(8,128)(2,1)}, bf16[64,2,16384]{2,0,1:T(8,128)(2,1)}, u32[]{:S(2)}, u32[]{:S(2)}) %collective-permute-start) | collective-permute-done | bytes 4194336 | tf_op jit(solution)/shard_map/ppermute | solution.py:23
  282.5 17.8 %copy.167 = bf16[64,2,16384]{0,1,2:T(2,128)(2,1)} copy(bf16[64,2,16384]{2,0,1:T(8,128)(2,1)} %collective-permute-done) | data formatting | bytes 8388608 | tf_op jit(solution)/shard_map/ppermute | solution.py:23
  300.2 39.0 %gather_fusion.3 = bf16[64,64,2,512]{1,2,3,0:T(2,128)(2,1)} fusion(bf16[64,2,16384]{0,1,2:T(2,128)(2,1)} %copy.167, s32[64]{0:T(128)S(1)} %reshape.255), kind=kCustom, calls=%fused_computation.3 | custom fusion | bytes 16777984 | tf_op jit(solution)/shard_map/vmap(vmap())/gather | solution.py:178
  339.2 33.8 %copy.168 = bf16[64,64,2,512]{3,1,0,2:T(8,128)(2,1)} copy(bf16[64,64,2,512]{1,2,3,0:T(2,128)(2,1)} %gather_fusion.3) | data formatting | bytes 16777216 | tf_op jit(solution)/shard_map/vmap(vmap())/gather | solution.py:178
  373.0 6.9 select_select_fusion
  390.4 8.1 %fusion.1 = bf16[16,4,64,1,512]{4,2,1,0,3:T(8,128)(2,1)} fusion(f32[16,4,64,512]{3,2,1,0:T(8,128)S(1)} %fusion.2, bf16[16,4,64,2,512]{4,2,1,0,3:T(8,128)(2,1)S(1)} %select_select_fusion), kind=kOutput, calls=%fused_computation.16 | convolution fusion | flops 2155872256 | bytes 16777216 | tf_op jit(solution)/shard_map/...cn,nf->...cf/dot_general | solution.py:46
  398.5 7.7 %fusion = bf16[16,4,64,1,512]{4,2,1,0,3:T(8,128)(2,1)} fusion(f32[16,4,64,512]{3,2,1,0:T(8,128)S(1)} %fusion.3, bf16[16,4,64,2,512]{4,2,1,0,3:T(8,128)(2,1)S(1)} %select_select_fusion), kind=kOutput, calls=%fused_computation.15 | convolution fusion | flops 2155872256 | bytes 16777216 | tf_op jit(solution)/shard_map/...cn,nf->...cf/dot_general | solution.py:46
  406.2 7.5 %pad_maximum_fusion.1 = bf16[16,4,64,2,512]{4,2,1,0,3:T(8,128)(2,1)} fusion(bf16[16,4,64,1,512]{4,2,1,0,3:T(8,128)(2,1)} %fusion.1, bf16[16,4,64,1,512]{4,2,1,0,3:T(8,128)(2,1)} %fusion), kind=kLoop, calls=%fused_computation.11 | loop fusion | flops 4194304 | bytes 16777216 | tf_op jit(solution)/shard_map/stack | solution.py:93
  413.7 7.7 %copy.170 = bf16[16,4,64,2,512]{4,2,1,3,0:T(8,128)(2,1)} copy(bf16[16,4,64,2,512]{4,2,1,0,3:T(8,128)(2,1)} %pad_maximum_fusion.1) | data formatting | bytes 16777216 | tf_op jit(solution)/shard_map/stack | solution.py:93
  428.4 110.5 %all-to-all-done.1 = bf16[16,4,64,2,512]{4,2,1,3,0:T(8,128)(2,1)} async-done(((bf16[16,4,64,2,512]{4,2,1,3,0:T(8,128)(2,1)}), bf16[16,4,64,2,512]{4,2,1,3,0:T(8,128)(2,1)}, u32[]{:S(2)}, u32[]{:S(2)}) %all-to-all-start.1) | async-done | bytes 8388640 | tf_op jit(solution)/shard_map/all_to_all | solution.py:191
  539.0 16.3 %copy.171 = bf16[16,4,64,2,512]{4,3,2,1,0:T(2,128)(2,1)} copy(bf16[16,4,64,2,512]{4,2,1,3,0:T(8,128)(2,1)} %all-to-all-done.1) | data formatting | bytes 16777216 | tf_op jit(solution)/shard_map/all_to_all | solution.py:191
  555.2 11.3 %reshape.233 = bf16[64,65536]{1,0:T(8,128)(2,1)} reshape(bf16[16,4,64,2,512]{4,3,2,1,0:T(2,128)(2,1)} %copy.171) | data formatting | bytes 16777216 | tf_op jit(solution)/shard_map/reshape | solution.py:146
  566.6 6.7 convolution_convert_fusion
  573.2 6.5 reshape.234
  579.7 20.1 %copy.173 = bf16[4,512,2,512]{1,2,0,3:T(2,128)(2,1)} copy(bf16[4,512,2,512]{3,2,1,0:T(2,128)(2,1)} %reshape.234) | data formatting | bytes 8388608 | tf_op jit(solution)/shard_map/reshape | solution.py:192
  (136 shorter events, 166.9 us)
Async XLA Ops:
  0.0 426.3 %copy-start = (s32[8,63,3]{1,0,2:T(8,128)S(1)}, s32[8,63,3]{1,0,2:T(8,128)}, u32[]{:S(2)}) copy-start(s32[8,63,3]{1,0,2:T(8,128)} %param.9) | copy-start | bytes 18148
  5.5 62.4 %all-to-all-start = ((bf16[16,64,2,1024]{3,1,2,0:T(8,128)(2,1)}), bf16[16,64,2,1024]{3,1,2,0:T(8,128)(2,1)}, u32[]{:S(2)}, u32[]{:S(2)}) async-start(bf16[16,64,2,1024]{3,1,2,0:T(8,128)(2,1)} %copy.150), calls=%async_computation | async-start | bytes 8388608 | tf_op jit(solution)/shard_map/all_to_all | solution.py:160
  83.0 2.2 copy-start.1
  83.0 3.5 copy-start.2
  113.2 17.3 %copy-start.3 = (bf16[64,1,16384]{2,0,1:T(8,128)(2,1)S(1)}, bf16[64,1,16384]{2,0,1:T(8,128)(2,1)}, u32[]{:S(2)}) copy-start(bf16[64,1,16384]{2,0,1:T(8,128)(2,1)} %stack_reshape.9) | copy-start | bytes 6291460
  185.5 97.0 %collective-permute-start = (bf16[64,2,16384]{2,0,1:T(8,128)(2,1)}, bf16[64,2,16384]{2,0,1:T(8,128)(2,1)}, u32[]{:S(2)}, u32[]{:S(2)}) collective-permute-start(bf16[64,2,16384]{2,0,1:T(8,128)(2,1)} %copy.161), channel_id=1, source_target_pairs={{16,0},{32,16},{48,32},{64,48},{80,64},{96,80},{112,96},{17,1},{33... | collective-permute-start | bytes 12582920 | tf_op jit(solution)/shard_map/ppermute | solution.py:23
  421.4 117.6 %all-to-all-start.1 = ((bf16[16,4,64,2,512]{4,2,1,3,0:T(8,128)(2,1)}), bf16[16,4,64,2,512]{4,2,1,3,0:T(8,128)(2,1)}, u32[]{:S(2)}, u32[]{:S(2)}) async-start(bf16[16,4,64,2,512]{4,2,1,3,0:T(8,128)(2,1)} %copy.170), calls=%async_computation.1 | async-start | bytes 16777216 | tf_op jit(solution)/shard_map/all_to_all | solution.py:191
  679.2 5.5 copy-start.5
  679.2 5.5 copy-start.7
  683.7 1.6 copy-start.4
  685.3 1.6 copy-start.6
where the time goes:
time: 699 us; the launch traced here: 691 us
  local copies, waits for them, and re-layouts  336 us (48%)
  waiting for transfers between devices  172 us (25%)
  matrix products  116 us (17%)
  other arithmetic  52.7 us (8%)
  starting transfers between devices  13.1 us (2%)
    all_to_all x1, waiting for transfers between devices, shards(): lax.all_to_all(sent_spectra, 'az', split_axis=0, concat_axis=0, tiled=True)  111 us
    dot_general x50, matrix products, mix(): return jnp.einsum(form, left, right, preferred_element_type=jnp.float32)  110 us
    gather x2, local copies, waits for them, and re-layouts, cut_block(): own_part = lax.dynamic_slice_in_dim(focused, first_line, IMG_L, 2)  72.8 us
    gather x2, local copies, waits for them, and re-layouts, cut_block(): next_part = lax.dynamic_slice_in_dim(beyond, first_line, IMG_L, 2)  72.8 us
    another operation x5, local copies, waits for them, and re-layouts, focus_turned(): jnp.stack([final_re.reshape(count, -1), final_im.reshape(count, -1)], axi...  55.9 us
    all_to_all x1, waiting for transfers between devices, shards(): lax.all_to_all(pieces, 'az', split_axis=0, concat_axis=0, tiled=True)  45.1 us
    reshape x2, local copies, waits for them, and re-layouts, shards(): images = assemble(arrived, selector).reshape(IMG_DEV, IMG_C, 2, IMG_L)  26.5 us
    another operation x1, other arithmetic, focus_turned(): jnp.stack([final_re.reshape(count, -1), final_im.reshape(count, -1)], axi...  24.7 us
  transfers between devices with their start and end apart: 3, of which 3 were waited for; matrix products, arithmetic and copies ran while one was open for 13% of the time, Pallas kernels for 0%

commit v1 on v0

v1 whole, which is shorter than its diff:
```python
import math

import jax
import jax.numpy as jnp
import numpy as np
from jax import lax
from jax.experimental import pallas as pl
from jax.experimental.pallas import tpu as pltpu
from jax.sharding import PartitionSpec as P

AZ_OUTER = 128
AZ_INNER = 128
LINES = 16384
IMG_C = 512
IMG_L = 512
LOOK = 128
COL = 64
IMG_DEV = 4
SPAN = IMG_C // COL
BLOCK = 8
TURN_ROWS = 16
epsilon = 1e-06
bf16 = jnp.bfloat16
f32 = jnp.float32


def dft_np(length, sign):
    steps = np.arange(length)
    phase = (steps[:, None] * steps[None, :]) % length
    angle = 2.0 * math.pi * phase / length
    scale = 1.0 / math.sqrt(length)
    return np.cos(angle) * scale, sign * np.sin(angle) * scale


def low(table):
    return np.asarray(table, np.float32).astype(jnp.bfloat16)


def left_form(length, sign):
    re, im = dft_np(length, sign)
    return low(np.block([[re, -im], [im, re]]))


def right_form(length, sign):
    re, im = dft_np(length, sign)
    return low(np.block([[re, im], [-im, re]]))


def twiddles():
    steps = np.arange(AZ_OUTER)
    angle = 2.0 * math.pi * ((steps[:, None] * steps[None, :]) % LINES) / LINES
    return np.stack([np.cos(angle), -np.sin(angle)]).astype(np.float32)


def dot(left, right):
    return jnp.dot(left, right, preferred_element_type=f32)


def focus_kernel(arr_ref, filt_ref, l1_ref, t2_ref, t3_ref, l4_ref, tw_ref, x_ref, y_ref, *, steps):
    step = pl.program_id(0)

    @pl.when(step < steps)
    def _():
        tw_re = tw_ref[0]
        tw_im = tw_ref[1]
        for pair in range(BLOCK // 2):
            cells = (2 * pair, 2 * pair + 1)

            def stacked(cell):
                return jnp.concatenate(
                    [arr_ref[:, cell, part].reshape(AZ_OUTER, AZ_INNER) for part in (0, 1)], axis=0
                )

            out = dot(l1_ref[...], jnp.concatenate([stacked(c) for c in cells], axis=1))
            rows = []
            for half in (0, 1):
                re = out[:128, half * 128 : half * 128 + 128]
                im = out[128:, half * 128 : half * 128 + 128]
                rows.append(
                    jnp.concatenate([re * tw_re - im * tw_im, re * tw_im + im * tw_re], axis=1)
                )
            section = jnp.concatenate(rows, axis=0).astype(bf16)
            out = dot(section, t2_ref[...])
            rows = []
            for half in (0, 1):
                re = out[half * 128 : half * 128 + 128, :128]
                im = out[half * 128 : half * 128 + 128, 128:]
                g_re = filt_ref[cells[half], 0].astype(f32)
                g_im = filt_ref[cells[half], 1].astype(f32)
                rows.append(jnp.concatenate([re * g_re - im * g_im, re * g_im + im * g_re], axis=1))
            spectrum = jnp.concatenate(rows, axis=0).astype(bf16)
            out = dot(spectrum, t3_ref[...])
            columns = []
            for half in (0, 1):
                re = out[half * 128 : half * 128 + 128, :128]
                im = out[half * 128 : half * 128 + 128, 128:]
                columns.append(
                    jnp.concatenate([re * tw_re + im * tw_im, im * tw_re - re * tw_im], axis=0)
                )
            out = dot(l4_ref[...], jnp.concatenate(columns, axis=1).astype(bf16))
            for half in (0, 1):
                cell = step * BLOCK + cells[half]
                y_ref[pl.ds(cell * 128, 128), :] = out[:128, half * 128 : half * 128 + 128]
                y_ref[pl.ds((COL + cell) * 128, 128), :] = out[128:, half * 128 : half * 128 + 128]

    @pl.when(step >= steps)
    def _():
        first = (step - steps) * TURN_ROWS
        for row in range(TURN_ROWS):
            block = y_ref[pl.ds(first + row, 128, stride=128), :]
            x_ref[row * 128 : row * 128 + 128, :] = block.T.astype(bf16)


def focus(arrived, response):
    steps = COL // BLOCK
    turns = AZ_OUTER // TURN_ROWS
    whole = lambda shape: pl.BlockSpec(shape, lambda i: (0,) * len(shape))
    return pl.pallas_call(
        lambda *refs: focus_kernel(*refs, steps=steps),
        out_shape=jax.ShapeDtypeStruct((LINES, 2 * COL), bf16),
        grid=(steps + turns,),
        in_specs=[
            pl.BlockSpec((16, BLOCK, 2, 8, 128), lambda i: (0, jnp.minimum(i, steps - 1), 0, 0, 0)),
            pl.BlockSpec((BLOCK, 2, 128, 128), lambda i: (jnp.minimum(i, steps - 1), 0, 0, 0)),
            whole((256, 256)),
            whole((256, 256)),
            whole((256, 256)),
            whole((256, 256)),
            whole((2, 128, 128)),
        ],
        out_specs=pl.BlockSpec((TURN_ROWS * 128, 128), lambda i: (jnp.maximum(i - steps, 0), 0)),
        scratch_shapes=[pltpu.VMEM((LINES, 128), f32)],
        name="focus",
    )(
        arrived,
        response,
        jnp.asarray(left_form(128, -1.0)),
        jnp.asarray(right_form(128, -1.0)),
        jnp.asarray(right_form(128, 1.0)),
        jnp.asarray(left_form(128, 1.0)),
        jnp.asarray(twiddles()),
    )


def turned(value, sign):
    return pltpu.roll(value, 64, 1) * sign


def powers_kernel(info_ref, *refs, resumed):
    if resumed:
        x_ref, w_ref, u_ref, old_ref, out_ref, lines_ref, spec_ref = refs
    else:
        x_ref, w_ref, u_ref, out_ref, lines_ref, spec_ref = refs
        old_ref = None
    owner = pl.program_id(0)
    lane = lax.broadcasted_iota(jnp.int32, (1, 128), 1)
    sign = jnp.where(lane < 64, -1.0, 1.0).astype(f32)

    @pl.when(owner == 0)
    def _():
        def widen(part, carry):
            rows = pl.ds(pl.multiple_of(part * 1024, 1024), 1024)
            lines_ref[rows, :] = x_ref[rows, :].astype(f32)
            return carry

        lax.fori_loop(0, LINES // 1024, widen, 0)

    for pair in range(2):
        slots = [owner * IMG_DEV + 2 * pair + half for half in (0, 1)]
        keeps = [info_ref[slot * 8 + 1] for slot in slots]

        if resumed:
            out_ref[0, pair] = old_ref[0, pair]

        @pl.when(keeps[0] + keeps[1] > 0)
        def _():
            columns = []
            for slot in slots:
                image = lines_ref[pl.ds(info_ref[slot * 8], IMG_L), :]
                columns.append(
                    jnp.concatenate([image.astype(bf16), turned(image, sign).astype(bf16)], axis=0)
                )
            spectra = dot(w_ref[...], jnp.concatenate(columns, axis=1))
            for half in (0, 1):
                spec_ref[half * IMG_L : half * IMG_L + IMG_L, :] = spectra[:, half * 128 : half * 128 + 128]
            for look in range(3):
                powers = []
                for half, slot in enumerate(slots):
                    band = spec_ref[pl.ds(half * IMG_L + info_ref[slot * 8 + 2 + look], LOOK), :]
                    both = jnp.concatenate([band.astype(bf16), turned(band, sign).astype(bf16)], axis=0)
                    value = dot(u_ref[...], both)
                    square = value * value
                    powers.append(square + pltpu.roll(square, 64, 1))
                power = jnp.where(lane < 64, powers[0], powers[1]).astype(bf16)
                if resumed:
                    fresh = jnp.where(lane < 64, keeps[0], keeps[1]) > 0
                    power = jnp.where(fresh, power.astype(f32), old_ref[0, pair, look].astype(f32)).astype(bf16)
                out_ref[0, pair, look] = power


def looks_of(info, lines, old=None):
    re, im = dft_np(IMG_L, -1.0)
    back_re, back_im = dft_np(LOOK, 1.0)
    whole = lambda shape: pl.BlockSpec(shape, lambda i, s: (0,) * len(shape))
    block = pl.BlockSpec((1, 2, 3, 128, 128), lambda i, s: (i, 0, 0, 0, 0))
    resumed = old is not None
    owners = 16
    return pl.pallas_call(
        lambda *refs: powers_kernel(*refs, resumed=resumed),
        out_shape=jax.ShapeDtypeStruct((owners, 2, 3, 128, 128), bf16),
        grid_spec=pltpu.PrefetchScalarGridSpec(
            num_scalar_prefetch=1,
            grid=(owners,),
            in_specs=[whole((LINES, 128)), whole((IMG_L, 2 * IMG_L)), whole((LOOK, 2 * LOOK))]
            + ([block] if resumed else []),
            out_specs=block,
            scratch_shapes=[pltpu.VMEM((LINES, 128), f32), pltpu.VMEM((2 * IMG_L, 128), f32)],
        ),
        name="looks_beyond" if resumed else "looks_own",
    )(
        info,
        lines,
        jnp.asarray(low(np.concatenate([re, im], axis=1))),
        jnp.asarray(low(np.concatenate([back_re, back_im], axis=1))),
        *([old] if resumed else []),
    )


def cross_kernel(info_ref, arr_ref, w_ref, l_ref, out_ref):
    pair = pl.program_id(0)
    lane = lax.broadcasted_iota(jnp.int32, (1, 128), 1)
    for half in (0, 1):
        slot = 2 * pair + half
        start = info_ref[slot * 2]
        filled = info_ref[slot * 2 + 1] > 0
        rows = []
        for look in range(3):
            pieces = []
            for part in range(SPAN // 2):
                ahead = arr_ref[(start + 2 * part) % 16, 0, look].astype(f32)
                after = arr_ref[(start + 2 * part + 1) % 16, 0, look].astype(f32)
                if half == 0:
                    after = pltpu.roll(after, 64, 1)
                else:
                    ahead = pltpu.roll(ahead, 64, 1)
                pieces.append(jnp.where(lane < 64, ahead, after))
            power = jnp.concatenate(pieces, axis=1)
            mean = jnp.sum(power) * (1.0 / (IMG_C * LOOK))
            rows.append((power / (mean + epsilon) - 1.0).astype(bf16))
        across = dot(jnp.concatenate(rows, axis=0), w_ref[...]).astype(bf16)
        waves = []
        for look in range(3):
            part = across[look * 128 : look * 128 + 128]
            both = jnp.concatenate([part[:, :IMG_C], part[:, IMG_C:]], axis=0)
            value = dot(l_ref[...], both)
            waves.append((value[:128], value[128:]))
        total_re = jnp.zeros((LOOK, IMG_C), f32)
        total_im = jnp.zeros((LOOK, IMG_C), f32)
        for first, second in ((0, 1), (1, 2), (0, 2)):
            one_re, one_im = waves[first]
            two_re, two_im = waves[second]
            total_re = total_re + one_re * two_re + one_im * two_im
            total_im = total_im + one_im * two_re - one_re * two_im
        out_ref[half, 0] = jnp.where(filled, total_re, 0.0).T
        out_ref[half, 1] = jnp.where(filled, total_im, 0.0).T


def cross(info, arrived):
    re, im = dft_np(IMG_C, -1.0)
    whole = lambda shape: pl.BlockSpec(shape, lambda i, s: (0,) * len(shape))
    return pl.pallas_call(
        cross_kernel,
        out_shape=jax.ShapeDtypeStruct((IMG_DEV, 2, IMG_C, LOOK), f32),
        grid_spec=pltpu.PrefetchScalarGridSpec(
            num_scalar_prefetch=1,
            grid=(2,),
            in_specs=[
                pl.BlockSpec((16, 1, 3, 128, 128), lambda i, s: (0, i, 0, 0, 0)),
                whole((IMG_C, 2 * IMG_C)),
                whole((256, 256)),
            ],
            out_specs=pl.BlockSpec((2, 2, IMG_C, LOOK), lambda i, s: (i, 0, 0, 0)),
        ),
        name="cross",
    )(info, arrived, jnp.asarray(low(np.concatenate([re, im], axis=1))), jnp.asarray(left_form(128, -1.0)))


def slot_info(anchors, owners, look_bands, strip, column, count):
    row = lax.dynamic_index_in_dim(owners, strip, 0, keepdims=False)
    facts = jnp.concatenate(
        [
            lax.dynamic_index_in_dim(anchors, strip, 0, keepdims=False),
            lax.dynamic_index_in_dim(look_bands, strip, 0, keepdims=False),
        ],
        axis=1,
    )
    items = jnp.arange(row.shape[0], dtype=jnp.int32)
    earlier = (row[:, None] == row[None, :]) & (items[None, :] < items[:, None])
    rank = jnp.sum(earlier.astype(jnp.int32), axis=1)
    place = row * IMG_DEV + rank
    slots = jnp.arange(count * IMG_DEV, dtype=jnp.int32)
    hot = (place[None, :] == slots[:, None]).astype(jnp.int32)
    filled = jnp.sum(hot, axis=1)
    chosen = jnp.sum(hot[:, :, None] * facts[None], axis=1)
    line = jnp.clip(chosen[:, 0], 0, LINES - IMG_L)
    start = chosen[:, 1]
    bands = jnp.clip(chosen[:, 2:], 0, IMG_L - LOOK)
    own = (start <= column) & (column < start + SPAN) & (filled > 0)
    shifted = column + count
    beyond = (start <= shifted) & (shifted < start + SPAN) & (filled > 0)
    pad = jnp.zeros((slots.shape[0], 3), jnp.int32)

    def listed(keep):
        return jnp.concatenate(
            [line[:, None], keep.astype(jnp.int32)[:, None], bands, pad], axis=1
        ).reshape(-1)

    mine = jnp.stack([start, filled], axis=1)
    mine = lax.dynamic_slice_in_dim(mine, column * IMG_DEV, IMG_DEV, 0).reshape(-1)
    return listed(own), listed(beyond), mine


def shards(raw_swath, azimuth_filter, anchors, owners, look_bands):
    count = lax.axis_size("az")
    strips = lax.axis_size("rng")
    strip = lax.axis_index("rng")
    column = lax.axis_index("az")
    own, beyond, mine = slot_info(anchors, owners, look_bands, strip, column, count)
    pieces = raw_swath.reshape(count, COL, 2, 8, 128)
    arrived = lax.all_to_all(pieces, "az", split_axis=0, concat_axis=0, tiled=True)
    lines = focus(arrived, azimuth_filter.reshape(COL, 2, AZ_OUTER, AZ_INNER))
    reach = [
        ((r + 1) * count + c, r * count + c) for r in range(strips - 1) for c in range(SPAN - 1)
    ]
    next_lines = lax.ppermute(lines, ("rng", "az"), reach)
    powers = looks_of(own, lines)
    powers = looks_of(beyond, next_lines, powers)
    powers = lax.all_to_all(powers, "az", split_axis=0, concat_axis=0, tiled=True)
    return cross(mine, powers)[None]


def solution(mesh):
    in_specs = (P("rng", None, "az"), P(("rng", "az"), None, None), P(), P(), P())
    out_specs = P("rng", "az", None, None, None)
    return jax.shard_map(shards, mesh=mesh, in_specs=in_specs, out_specs=out_specs, check_vma=False)
```

time: 699 us -> 278 us (0.40)
  local copies, waits for them, and re-layouts: 336 us -> 20.9 us
  matrix products: 116 us -> 0 us
  Pallas kernels: 0 us -> 78.6 us
  other arithmetic: 52.7 us -> 1.23 us
  waiting for transfers between devices: 172 us -> 159 us
    gather x13 -> x0, local copies, waits for them, and re-layouts: 164 us -> none  [the longest x2 72.8 us: cut_block(): own_part = lax.dynamic_slice_in_dim(focused, first_line, IMG_L, 2)]
    dot_general x51 -> x0, matrix products: 116 us -> none  [the longest x50 110 us: mix(): return jnp.einsum(form, left, right, preferred_element_type=jnp.float32)]
    pallas_call x0 -> x4, Pallas kernels: none -> 78.6 us  [the longest x2 47.1 us: looks_of(): pl.pallas_call(lambda *refs: powers_kernel(*refs, resumed=resumed), out_s...]
    all_to_all x1, waiting for transfers between devices: 111 us -> 41.8 us  [shards(): lax.all_to_all(powers, 'az', split_axis=0, concat_axis=0, tiled=True)]
    another operation x6 -> x0, local copies, waits for them, and re-layouts: 63.7 us -> none  [the longest x5 55.9 us: focus_turned(): jnp.stack([final_re.reshape(count, -1), final_im.reshape(count, -1)], axi...]
    ppermute x1, waiting for transfers between devices: 16.4 us -> 67.9 us  [shards(): next_lines = lax.ppermute(lines, ('rng', 'az'), reach)]
    another operation x3 -> x1, other arithmetic: 32.2 us -> 0.01 us  [slot_info(): mine = jnp.stack([start, filled], axis=1)]
    reshape x4 -> x5, local copies, waits for them, and re-layouts: 43.4 us -> 17.5 us  [the longest x1 7.9 us: shards(): lines = focus(arrived, azimuth_filter.reshape(COL, 2, AZ_OUTER, AZ_INNER))]
  transfers between devices with their start and end apart: 3 -> 3, of which waited for: 3 -> 3; matrix products, arithmetic and copies ran while one was open for 13% -> 5% of each run, Pallas kernels for 0% -> 8%
where the time goes in v1:
time: 278 us; the launch traced here: 274 us
  waiting for transfers between devices  159 us (57%)
  Pallas kernels  78.6 us (28%)
  local copies, waits for them, and re-layouts  20.9 us (8%)
  starting transfers between devices  14.2 us (5%)
    ppermute x1, waiting for transfers between devices, shards(): next_lines = lax.ppermute(lines, ('rng', 'az'), reach)  67.9 us
    all_to_all x1, waiting for transfers between devices, shards(): lax.all_to_all(pieces, 'az', split_axis=0, concat_axis=0, tiled=True)  49 us
    pallas_call x2, Pallas kernels, looks_of(): pl.pallas_call(lambda *refs: powers_kernel(*refs, resumed=resumed), out_s...  47.1 us
    all_to_all x1, waiting for transfers between devices, shards(): lax.all_to_all(powers, 'az', split_axis=0, concat_axis=0, tiled=True)  41.8 us
    pallas_call x1, Pallas kernels, focus(): pl.pallas_call(lambda *refs: focus_kernel(*refs, steps=steps), out_shape=...  23.4 us
    pallas_call x1, Pallas kernels, cross(): pl.pallas_call(cross_kernel, out_shape=jax.ShapeDtypeStruct((IMG_DEV, 2,...  8.06 us
    reshape x1, local copies, waits for them, and re-layouts, shards(): lines = focus(arrived, azimuth_filter.reshape(COL, 2, AZ_OUTER, AZ_INNER))  7.9 us
    reshape x1, local copies, waits for them, and re-layouts, shards(): pieces = raw_swath.reshape(count, COL, 2, 8, 128)  7.59 us
  transfers between devices with their start and end apart: 3, of which 3 were waited for; matrix products, arithmetic and copies ran while one was open for 5% of the time, Pallas kernels for 8%

profile of v1, /device:TPU:50, one launch (start us, length us, event | category | flops | bytes accessed | tf_op | source)
XLA Modules:
  0.0 273.8 jit_solution(13719087597539053319)
XLA Ops:
  0.0 7.6 %reshape.50 = bf16[16,64,2,8,128]{4,3,2,1,0:T(8,128)(2,1)} reshape(bf16[1024,2,1024]{2,1,0:T(2,128)(2,1)} %param.16) | data formatting | bytes 8388608 | tf_op jit(solution)/shard_map/reshape | solution.py:329
  7.6 5.6 %all-to-all-start = ((bf16[16,64,2,8,128]{4,3,2,1,0:T(8,128)(2,1)}), bf16[16,64,2,8,128]{4,3,2,1,0:T(8,128)(2,1)}, u32[]{:S(2)}, u32[]{:S(2)}) async-start(bf16[16,64,2,8,128]{4,3,2,1,0:T(8,128)(2,1)} %reshape.50), calls=%async_computation | async-start | bytes 8388608 | tf_op jit(solution)/shard_map/all_to_all | solution.py:330
  13.2 7.9 %reshape.51.refs_1_ = bf16[64,2,128,128]{3,2,1,0:T(8,128)(2,1)} reshape(bf16[64,2,16384]{2,1,0:T(2,128)(2,1)} %param.17) | data formatting | bytes 8388608 | tf_op jit(solution)/shard_map/reshape | solution.py:331
  21.1 49.0 %all-to-all-done.refs_0_ = bf16[16,64,2,8,128]{4,3,2,1,0:T(8,128)(2,1)} async-done(((bf16[16,64,2,8,128]{4,3,2,1,0:T(8,128)(2,1)}), bf16[16,64,2,8,128]{4,3,2,1,0:T(8,128)(2,1)}, u32[]{:S(2)}, u32[]{:S(2)}) %all-to-all-start) | async-done | bytes 4194336 | tf_op jit(solution)/shard_map/all_to_all | solution.py:330
  70.0 23.4 %focus.1.refs_1_ = bf16[16384,128]{1,0:T(8,128)(2,1)} custom-call(bf16[16,64,2,8,128]{4,3,2,1,0:T(8,128)(2,1)} %all-to-all-done.refs_0_, bf16[64,2,128,128]{3,2,1,0:T(8,128)(2,1)} %reshape.51.refs_1_, bf16[256,256]{1,0:T(8,128)(2,1)} %constant.48.clone.refs_2_.refs_4_.l_ref, bf16[256,256]{1,0:T(8,128)(2,1)} %constant.49.clone.refs_3_.refs_5_, ...), custom_call_target="tpu_custom_call" | custom-call | tf_op jit(solution)/shard_map/focus/pallas_call | solution.py:118
  93.5 2.5 collective-permute-start
  96.0 0.7 fusion.4
  96.7 0.7 dynamic-slice_bitcast_fusion
  97.4 0.2 convert_reduce_fusion
  97.6 0.7 fusion.3
  98.3 0.1 fusion.2
  98.4 0.2 multiply_reduce_fusion
  98.7 0.1 copy.25
  98.8 0.7 reshape.52.refs_0_
  99.5 0.7 reshape.49.refs_0_
  100.2 22.3 %looks_own.1.refs_4_ = bf16[16,2,3,128,128]{4,3,2,1,0:T(8,128)(2,1)} custom-call(s32[512]{0:T(512)} %reshape.52.refs_0_, bf16[16384,128]{1,0:T(8,128)(2,1)} %focus.1.refs_1_, bf16[512,1024]{1,0:T(8,128)(2,1)} %constant.51.clone.refs_2_.w_ref, bf16[128,256]{1,0:T(8,128)(2,1)} %constant.52.clone.refs_3_), custom_call_target="tpu_custom_call" | custom-call | tf_op jit(solution)/shard_map/looks_own/pallas_call | solution.py:208
  122.5 67.9 %collective-permute-done.refs_1_ = bf16[16384,128]{1,0:T(8,128)(2,1)} collective-permute-done((bf16[16384,128]{1,0:T(8,128)(2,1)}, bf16[16384,128]{1,0:T(8,128)(2,1)}, u32[]{:S(2)}, u32[]{:S(2)}) %collective-permute-start) | collective-permute-done | bytes 4194336 | tf_op jit(solution)/shard_map/ppermute | solution.py:335
  190.5 24.8 %looks_beyond.1 = bf16[16,2,3,128,128]{4,3,2,1,0:T(8,128)(2,1)} custom-call(s32[512]{0:T(512)} %reshape.49.refs_0_, bf16[16384,128]{1,0:T(8,128)(2,1)} %collective-permute-done.refs_1_, bf16[512,1024]{1,0:T(8,128)(2,1)} %constant.51.clone.refs_2_.w_ref, bf16[128,256]{1,0:T(8,128)(2,1)} %constant.52.clone.refs_3_, bf16[16,2,3,128,128]{4,3,2,1,0:T(8,128)(2,1)} %looks_own.1.refs_4_), custom_call_target="tpu_custom_call" | custom-call | tf_op jit(solution)/shard_map/looks_beyond/pallas_call | solution.py:208
  215.3 6.1 %all-to-all-start.1 = ((bf16[16,2,3,128,128]{4,3,2,1,0:T(8,128)(2,1)}), bf16[16,2,3,128,128]{4,3,2,1,0:T(8,128)(2,1)S(1)}, u32[]{:S(2)}, u32[]{:S(2)}) async-start(bf16[16,2,3,128,128]{4,3,2,1,0:T(8,128)(2,1)} %looks_beyond.1), calls=%async_computation.1 | async-start | bytes 6291456 | tf_op jit(solution)/shard_map/all_to_all | solution.py:338
  221.5 0.1 copy.23
  221.6 0.7 reshape.48.info_ref
  222.3 41.8 %all-to-all-done.1.arr_ref = bf16[16,2,3,128,128]{4,3,2,1,0:T(8,128)(2,1)S(1)} async-done(((bf16[16,2,3,128,128]{4,3,2,1,0:T(8,128)(2,1)}), bf16[16,2,3,128,128]{4,3,2,1,0:T(8,128)(2,1)S(1)}, u32[]{:S(2)}, u32[]{:S(2)}) %all-to-all-start.1) | async-done | bytes 3145760 | tf_op jit(solution)/shard_map/all_to_all | solution.py:338
  264.1 1.7 copy-done.1
  265.8 8.1 %cross.1 = f32[4,2,512,128]{3,2,1,0:T(8,128)} custom-call(s32[8]{0:T(128)} %reshape.48.info_ref, bf16[16,2,3,128,128]{4,3,2,1,0:T(8,128)(2,1)} %copy-done.1, bf16[512,1024]{1,0:T(8,128)(2,1)} %constant.51.clone.refs_2_.w_ref, bf16[256,256]{1,0:T(8,128)(2,1)} %constant.48.clone.refs_2_.refs_4_.l_ref), custom_call_target="tpu_custom_call" | custom-call | tf_op jit(solution)/shard_map/cross/pallas_call | solution.py:271
  (15 shorter events, 0.2 us)
Async XLA Ops:
  0.0 96.0 %copy-start = (s32[8,63,3]{1,0,2:T(8,128)S(1)}, s32[8,63,3]{1,0,2:T(8,128)}, u32[]{:S(2)}) copy-start(s32[8,63,3]{1,0,2:T(8,128)} %param.20) | copy-start | bytes 18148
  7.6 62.4 %all-to-all-start = ((bf16[16,64,2,8,128]{4,3,2,1,0:T(8,128)(2,1)}), bf16[16,64,2,8,128]{4,3,2,1,0:T(8,128)(2,1)}, u32[]{:S(2)}, u32[]{:S(2)}) async-start(bf16[16,64,2,8,128]{4,3,2,1,0:T(8,128)(2,1)} %reshape.50), calls=%async_computation | async-start | bytes 8388608 | tf_op jit(solution)/shard_map/all_to_all | solution.py:330
  93.5 97.0 %collective-permute-start = (bf16[16384,128]{1,0:T(8,128)(2,1)}, bf16[16384,128]{1,0:T(8,128)(2,1)}, u32[]{:S(2)}, u32[]{:S(2)}) collective-permute-start(bf16[16384,128]{1,0:T(8,128)(2,1)} %focus.1.refs_1_), channel_id=1, source_target_pairs={{16,0},{17,1},{18,2},{19,3},{20,4},{21,5},{22,6},{32,16},{33,17},{... | collective-permute-start | bytes 12582920 | tf_op jit(solution)/shard_map/ppermute | solution.py:335
  215.3 48.8 %all-to-all-start.1 = ((bf16[16,2,3,128,128]{4,3,2,1,0:T(8,128)(2,1)}), bf16[16,2,3,128,128]{4,3,2,1,0:T(8,128)(2,1)S(1)}, u32[]{:S(2)}, u32[]{:S(2)}) async-start(bf16[16,2,3,128,128]{4,3,2,1,0:T(8,128)(2,1)} %looks_beyond.1), calls=%async_computation.1 | async-start | bytes 6291456 | tf_op jit(solution)/shard_map/all_to_all | solution.py:338
  264.1 1.7 copy-start.1

commit v2 on v1

--- a/solution.py
+++ b/solution.py
@@ -7,6 +7,7 @@
 from jax.experimental import pallas as pl
 from jax.experimental.pallas import tpu as pltpu
 from jax.sharding import PartitionSpec as P
+
 
 AZ_OUTER = 128
 AZ_INNER = 128
@@ -19,6 +20,7 @@
 SPAN = IMG_C // COL
 BLOCK = 8
 TURN_ROWS = 16
+MERGED = 4
 epsilon = 1e-06
 bf16 = jnp.bfloat16
 f32 = jnp.float32
@@ -146,17 +148,25 @@
     return pltpu.roll(value, 64, 1) * sign
 
 
-def powers_kernel(info_ref, *refs, resumed):
-    if resumed:
-        x_ref, w_ref, u_ref, old_ref, out_ref, lines_ref, spec_ref = refs
-    else:
-        x_ref, w_ref, u_ref, out_ref, lines_ref, spec_ref = refs
-        old_ref = None
-    owner = pl.program_id(0)
+def looks_kernel(info_ref, x_ref, w_ref, u_ref, *refs, pair, split, skipped):
+    refs = refs[skipped:]
+    outs = refs[: 2 if split else 1]
+    lines_ref, spec_ref, list_ref = refs[len(outs) :]
+    owners = 16
     lane = lax.broadcasted_iota(jnp.int32, (1, 128), 1)
     sign = jnp.where(lane < 64, -1.0, 1.0).astype(f32)
-
-    @pl.when(owner == 0)
+    counts = []
+    for half in (0, 1):
+        for place in range(20):
+            list_ref[half * 20 + place] = 0
+        found = 0
+        for owner in range(owners):
+            list_ref[half * 20 + found] = owner
+            found = found + info_ref[(owner * IMG_DEV + 2 * pair + half) * 8 + 1]
+        counts.append(found)
+    trips = (jnp.maximum(counts[0], counts[1]) + 1) // 2
+
+    @pl.when(trips > 0)
     def _():
         def widen(part, carry):
             rows = pl.ds(pl.multiple_of(part * 1024, 1024), 1024)
@@ -165,69 +175,106 @@
 
         lax.fori_loop(0, LINES // 1024, widen, 0)
 
-    for pair in range(2):
-        slots = [owner * IMG_DEV + 2 * pair + half for half in (0, 1)]
-        keeps = [info_ref[slot * 8 + 1] for slot in slots]
-
-        if resumed:
-            out_ref[0, pair] = old_ref[0, pair]
-
-        @pl.when(keeps[0] + keeps[1] > 0)
-        def _():
-            columns = []
-            for slot in slots:
-                image = lines_ref[pl.ds(info_ref[slot * 8], IMG_L), :]
-                columns.append(
-                    jnp.concatenate([image.astype(bf16), turned(image, sign).astype(bf16)], axis=0)
-                )
-            spectra = dot(w_ref[...], jnp.concatenate(columns, axis=1))
-            for half in (0, 1):
-                spec_ref[half * IMG_L : half * IMG_L + IMG_L, :] = spectra[:, half * 128 : half * 128 + 128]
-            for look in range(3):
-                powers = []
-                for half, slot in enumerate(slots):
-                    band = spec_ref[pl.ds(half * IMG_L + info_ref[slot * 8 + 2 + look], LOOK), :]
-                    both = jnp.concatenate([band.astype(bf16), turned(band, sign).astype(bf16)], axis=0)
-                    value = dot(u_ref[...], both)
-                    square = value * value
-                    powers.append(square + pltpu.roll(square, 64, 1))
-                power = jnp.where(lane < 64, powers[0], powers[1]).astype(bf16)
-                if resumed:
-                    fresh = jnp.where(lane < 64, keeps[0], keeps[1]) > 0
-                    power = jnp.where(fresh, power.astype(f32), old_ref[0, pair, look].astype(f32)).astype(bf16)
-                out_ref[0, pair, look] = power
-
-
-def looks_of(info, lines, old=None):
+        def trip(at, carry):
+            groups = [[(half, list_ref[half * 20 + 2 * at + nth]) for half in (0, 1)] for nth in (0, 1)]
+            for nth, group in enumerate(groups):
+                columns = []
+                for half, owner in group:
+                    first = info_ref[(owner * IMG_DEV + 2 * pair + half) * 8]
+                    image = lines_ref[pl.ds(first, IMG_L), :]
+                    columns.append(
+                        jnp.concatenate([image.astype(bf16), turned(image, sign).astype(bf16)], axis=0)
+                    )
+                spectra = dot(w_ref[...], jnp.concatenate(columns, axis=1))
+                for half in (0, 1):
+                    top = (2 * nth + half) * IMG_L
+                    spec_ref[top : top + IMG_L, :] = spectra[:, half * 128 : half * 128 + 128]
+            for nth, group in enumerate(groups):
+                for look in range(3):
+                    columns = []
+                    for half, owner in group:
+                        band = info_ref[(owner * IMG_DEV + 2 * pair + half) * 8 + 2 + look]
+                        value = spec_ref[pl.ds((2 * nth + half) * IMG_L + band, LOOK), :]
+                        columns.append(
+                            jnp.concatenate([value.astype(bf16), turned(value, sign).astype(bf16)], axis=0)
+                        )
+                    value = dot(u_ref[...], jnp.concatenate(columns, axis=1))
+                    for half, owner in group:
+                        square = value[:, half * 128 : half * 128 + 128]
+                        square = square * square
+                        power = (square + pltpu.roll(square, 64, 1)).astype(bf16)
+                        lanes = slice(half * 64, half * 64 + 64)
+                        if split:
+                            outs[0][owner, look, :, lanes] = power[:64, lanes]
+                            outs[1][owner, look, :, lanes] = power[64:, lanes]
+                        else:
+                            outs[0][owner, look, :, lanes] = power[:, lanes]
+            return carry
+
+        lax.fori_loop(0, trips, trip, 0)
+
+
+def looks_of(info, lines, pair, split, after=()):
     re, im = dft_np(IMG_L, -1.0)
     back_re, back_im = dft_np(LOOK, 1.0)
     whole = lambda shape: pl.BlockSpec(shape, lambda i, s: (0,) * len(shape))
-    block = pl.BlockSpec((1, 2, 3, 128, 128), lambda i, s: (i, 0, 0, 0, 0))
-    resumed = old is not None
     owners = 16
+    rows = LOOK // 2 if split else LOOK
+    shape = (owners, 3, rows, 128)
     return pl.pallas_call(
-        lambda *refs: powers_kernel(*refs, resumed=resumed),
-        out_shape=jax.ShapeDtypeStruct((owners, 2, 3, 128, 128), bf16),
+        lambda *refs: looks_kernel(*refs, pair=pair, split=split, skipped=len(after)),
+        out_shape=[jax.ShapeDtypeStruct(shape, bf16)] * (2 if split else 1),
         grid_spec=pltpu.PrefetchScalarGridSpec(
             num_scalar_prefetch=1,
-            grid=(owners,),
+            grid=(1,),
             in_specs=[whole((LINES, 128)), whole((IMG_L, 2 * IMG_L)), whole((LOOK, 2 * LOOK))]
-            + ([block] if resumed else []),
-            out_specs=block,
-            scratch_shapes=[pltpu.VMEM((LINES, 128), f32), pltpu.VMEM((2 * IMG_L, 128), f32)],
+            + [pl.BlockSpec(memory_space=pl.ANY)] * len(after),
+            out_specs=[whole(shape)] * (2 if split else 1),
+            scratch_shapes=[
+                pltpu.VMEM((LINES, 128), f32),
+                pltpu.VMEM((4 * IMG_L, 128), f32),
+                pltpu.SMEM((40,), jnp.int32),
+            ],
         ),
-        name="looks_beyond" if resumed else "looks_own",
     )(
         info,
         lines,
         jnp.asarray(low(np.concatenate([re, im], axis=1))),
         jnp.asarray(low(np.concatenate([back_re, back_im], axis=1))),
-        *([old] if resumed else []),
+        *after,
     )
 
 
-def cross_kernel(info_ref, arr_ref, w_ref, l_ref, out_ref):
-    pair = pl.program_id(0)
+def merge_kernel(flag_ref, own_ref, low_ref, high_ref, *refs, pair):
+    out_ref = refs[-1]
+    step = pl.program_id(0)
+    lane = lax.broadcasted_iota(jnp.int32, (1, 1, 128), 2)
+    for at in range(MERGED):
+        slot = (step * MERGED + at) * IMG_DEV + 2 * pair
+        for part, other_ref in enumerate((low_ref, high_ref)):
+            rows = slice(part * 64, part * 64 + 64)
+            flags = [flag_ref[(slot + half) * 2 + part] for half in (0, 1)]
+            taken = jnp.where(lane < 64, flags[0], flags[1]) > 0
+            own = own_ref[at, :, rows].astype(f32)
+            out_ref[at, :, rows] = jnp.where(taken, other_ref[at].astype(f32), own).astype(bf16)
+
+
+def merged(flags, own, low_rows, high_rows, pair, after=()):
+    block = lambda rows: pl.BlockSpec((MERGED, 3, rows, 128), lambda i, s: (i, 0, 0, 0))
+    return pl.pallas_call(
+        lambda *refs: merge_kernel(*refs, pair=pair),
+        out_shape=jax.ShapeDtypeStruct(own.shape, bf16),
+        grid_spec=pltpu.PrefetchScalarGridSpec(
+            num_scalar_prefetch=1,
+            grid=(16 // MERGED,),
+            in_specs=[block(128), block(64), block(64)] + [pl.BlockSpec(memory_space=pl.ANY)] * len(after),
+            out_specs=block(128),
+        ),
+    )(flags, own, low_rows, high_rows, *after)
+
+
+def cross_kernel(info_ref, arr_ref, w_ref, l_ref, *refs, pair):
+    out_ref = refs[-1]
     lane = lax.broadcasted_iota(jnp.int32, (1, 128), 1)
     for half in (0, 1):
         slot = 2 * pair + half
@@ -235,10 +282,17 @@
         filled = info_ref[slot * 2 + 1] > 0
         rows = []
         for look in range(3):
+
+            def piece(at):
+                column = start + at
+                top = arr_ref[column % 16, look, :64]
+                bottom = arr_ref[jnp.where(column < 16, column, column - 8), look, 64:]
+                return jnp.concatenate([top, bottom], axis=0).astype(f32)
+
             pieces = []
             for part in range(SPAN // 2):
-                ahead = arr_ref[(start + 2 * part) % 16, 0, look].astype(f32)
-                after = arr_ref[(start + 2 * part + 1) % 16, 0, look].astype(f32)
+                ahead = piece(2 * part)
+                after = piece(2 * part + 1)
                 if half == 0:
                     after = pltpu.roll(after, 64, 1)
                 else:
@@ -265,27 +319,35 @@
         out_ref[half, 1] = jnp.where(filled, total_im, 0.0).T
 
 
-def cross(info, arrived):
+def cross(info, arrived, pair, earlier=None):
     re, im = dft_np(IMG_C, -1.0)
     whole = lambda shape: pl.BlockSpec(shape, lambda i, s: (0,) * len(shape))
+    more = [] if earlier is None else [earlier]
     return pl.pallas_call(
-        cross_kernel,
+        lambda *refs: cross_kernel(*refs, pair=pair),
         out_shape=jax.ShapeDtypeStruct((IMG_DEV, 2, IMG_C, LOOK), f32),
         grid_spec=pltpu.PrefetchScalarGridSpec(
             num_scalar_prefetch=1,
-            grid=(2,),
+            grid=(1,),
             in_specs=[
-                pl.BlockSpec((16, 1, 3, 128, 128), lambda i, s: (0, i, 0, 0, 0)),
+                whole((16, 3, 128, 128)),
                 whole((IMG_C, 2 * IMG_C)),
                 whole((256, 256)),
-            ],
-            out_specs=pl.BlockSpec((2, 2, IMG_C, LOOK), lambda i, s: (i, 0, 0, 0)),
+            ]
+            + [pl.BlockSpec(memory_space=pl.ANY)] * len(more),
+            out_specs=pl.BlockSpec((2, 2, IMG_C, LOOK), lambda i, s: (pair, 0, 0, 0)),
         ),
-        name="cross",
-    )(info, arrived, jnp.asarray(low(np.concatenate([re, im], axis=1))), jnp.asarray(left_form(128, -1.0)))
-
-
-def slot_info(anchors, owners, look_bands, strip, column, count):
+        input_output_aliases={4: 0} if more else {},
+    )(
+        info,
+        arrived,
+        jnp.asarray(low(np.concatenate([re, im], axis=1))),
+        jnp.asarray(left_form(128, -1.0)),
+        *more,
+    )
+
+
+def strip_facts(anchors, owners, look_bands, strip, count):
     row = lax.dynamic_index_in_dim(owners, strip, 0, keepdims=False)
     facts = jnp.concatenate(
         [
@@ -303,43 +365,70 @@
     filled = jnp.sum(hot, axis=1)
     chosen = jnp.sum(hot[:, :, None] * facts[None], axis=1)
     line = jnp.clip(chosen[:, 0], 0, LINES - IMG_L)
-    start = chosen[:, 1]
     bands = jnp.clip(chosen[:, 2:], 0, IMG_L - LOOK)
-    own = (start <= column) & (column < start + SPAN) & (filled > 0)
-    shifted = column + count
-    beyond = (start <= shifted) & (shifted < start + SPAN) & (filled > 0)
-    pad = jnp.zeros((slots.shape[0], 3), jnp.int32)
-
-    def listed(keep):
-        return jnp.concatenate(
-            [line[:, None], keep.astype(jnp.int32)[:, None], bands, pad], axis=1
-        ).reshape(-1)
-
-    mine = jnp.stack([start, filled], axis=1)
-    mine = lax.dynamic_slice_in_dim(mine, column * IMG_DEV, IMG_DEV, 0).reshape(-1)
-    return listed(own), listed(beyond), mine
-
-
-def shards(raw_swath, azimuth_filter, anchors, owners, look_bands):
+    return line, chosen[:, 1], bands, filled
+
+
+def reaches(start, filled, column):
+    return ((start <= column) & (column < start + SPAN) & (filled > 0)).astype(jnp.int32)
+
+
+def listed(line, bands, keep):
+    pad = jnp.zeros((keep.shape[0], 3), jnp.int32)
+    return jnp.concatenate([line[:, None], keep[:, None], bands, pad], axis=1).reshape(-1)
+
+
+def staged(raw_swath, azimuth_filter, anchors, owners, look_bands):
     count = lax.axis_size("az")
     strips = lax.axis_size("rng")
     strip = lax.axis_index("rng")
     column = lax.axis_index("az")
-    own, beyond, mine = slot_info(anchors, owners, look_bands, strip, column, count)
+    line, start, bands, filled = strip_facts(anchors, owners, look_bands, strip, count)
+    own = listed(line, bands, reaches(start, filled, column))
+    flags = jnp.stack(
+        [
+            reaches(start, filled, column + count),
+            reaches(start, filled, column + SPAN) * (column >= SPAN).astype(jnp.int32),
+        ],
+        axis=1,
+    ).reshape(-1)
+    mine = jnp.stack([start, filled], axis=1)
+    mine = lax.dynamic_slice_in_dim(mine, column * IMG_DEV, IMG_DEV, 0).reshape(-1)
+    line, start, bands, filled = strip_facts(
+        anchors, owners, look_bands, jnp.maximum(strip - 1, 0), count
+    )
+    keep = reaches(start, filled, column + count) * (strip > 0).astype(jnp.int32)
+    beyond = listed(line, bands, keep)
+
     pieces = raw_swath.reshape(count, COL, 2, 8, 128)
     arrived = lax.all_to_all(pieces, "az", split_axis=0, concat_axis=0, tiled=True)
     lines = focus(arrived, azimuth_filter.reshape(COL, 2, AZ_OUTER, AZ_INNER))
     reach = [
-        ((r + 1) * count + c, r * count + c) for r in range(strips - 1) for c in range(SPAN - 1)
+        [((r + 1) * count + c, r * count + c + shift) for r in range(strips - 1) for c in range(SPAN - 1)]
+        for shift in (0, SPAN)
     ]
-    next_lines = lax.ppermute(lines, ("rng", "az"), reach)
-    powers = looks_of(own, lines)
-    powers = looks_of(beyond, next_lines, powers)
-    powers = lax.all_to_all(powers, "az", split_axis=0, concat_axis=0, tiled=True)
-    return cross(mine, powers)[None]
+    passed = []
+    after = ()
+    for pair in (0, 1):
+        parts = looks_of(beyond, lines, pair, True, after)
+        after = (parts[0],)
+        sent = []
+        for way in (0, 1):
+            sent.append(lax.ppermute(parts[way], ("rng", "az"), reach[way]))
+        passed.append(sent)
+    kept = []
+    for pair in (0, 1):
+        kept += looks_of(own, lines, pair, False, after)
+        after = (kept[-1],)
+    result = None
+    for pair in (0, 1):
+        powers = merged(flags, kept[pair], *passed[pair], pair, after)
+        powers = lax.all_to_all(powers, "az", split_axis=0, concat_axis=0, tiled=True)
+        result = cross(mine, powers, pair, result)
+    return result[None]
 
 
 def solution(mesh):
     in_specs = (P("rng", None, "az"), P(("rng", "az"), None, None), P(), P(), P())
     out_specs = P("rng", "az", None, None, None)
-    return jax.shard_map(shards, mesh=mesh, in_specs=in_specs, out_specs=out_specs, check_vma=False)
+    return jax.shard_map(staged, mesh=mesh, in_specs=in_specs, out_specs=out_specs, check_vma=False)

time: 278 us -> 228 us (0.82)
  the two profiles are of different devices: /device:TPU:50 before, /device:TPU:96 now
where the time goes in v2:
time: 228 us; the launch traced here: 227 us
  waiting for transfers between devices  95 us (42%)
  Pallas kernels  81.6 us (36%)
  starting transfers between devices  26.2 us (11%)
  local copies, waits for them, and re-layouts  23 us (10%)
    all_to_all x1, waiting for transfers between devices, staged(): lax.all_to_all(pieces, 'az', split_axis=0, concat_axis=0, tiled=True)  44.9 us
    pallas_call x4, Pallas kernels, looks_of(): pl.pallas_call(lambda *refs: looks_kernel(*refs, pair=pair, split=split,...  37.3 us
    ppermute x4, waiting for transfers between devices, staged(): sent.append(lax.ppermute(parts[way], ('rng', 'az'), reach[way]))  34.4 us
    pallas_call x1, Pallas kernels, focus(): pl.pallas_call(lambda *refs: focus_kernel(*refs, steps=steps), out_shape=...  23.6 us
    all_to_all x2, waiting for transfers between devices, staged(): lax.all_to_all(powers, 'az', split_axis=0, concat_axis=0, tiled=True)  15.6 us
    pallas_call x2, Pallas kernels, cross(): pl.pallas_call(lambda *refs: cross_kernel(*refs, pair=pair), out_shape=ja...  11.4 us
    ppermute x4, starting transfers between devices, staged(): sent.append(lax.ppermute(parts[way], ('rng', 'az'), reach[way]))  10.7 us
    all_to_all x2, starting transfers between devices, staged(): lax.all_to_all(powers, 'az', split_axis=0, concat_axis=0, tiled=True)  9.88 us
  transfers between devices with their start and end apart: 7, of which 4 were waited for; matrix products, arithmetic and copies ran while one was open for 6% of the time, Pallas kernels for 16%

profile of v2, /device:TPU:96, one launch (start us, length us, event | category | flops | bytes accessed | tf_op | source)
XLA Modules:
  0.0 227.0 jit_solution(14992941294353020108)
XLA Ops:
  0.0 7.6 %reshape.89 = bf16[16,64,2,8,128]{4,3,2,1,0:T(8,128)(2,1)} reshape(bf16[1024,2,1024]{2,1,0:T(2,128)(2,1)} %param.22) | data formatting | bytes 8388608 | tf_op jit(solution)/shard_map/reshape | solution.py:403
  7.6 5.6 %all-to-all-start = ((bf16[16,64,2,8,128]{4,3,2,1,0:T(8,128)(2,1)}), bf16[16,64,2,8,128]{4,3,2,1,0:T(8,128)(2,1)}, u32[]{:S(2)}, u32[]{:S(2)}) async-start(bf16[16,64,2,8,128]{4,3,2,1,0:T(8,128)(2,1)} %reshape.89), calls=%async_computation | async-start | bytes 8388608 | tf_op jit(solution)/shard_map/all_to_all | solution.py:404
  16.6 7.9 %reshape.90.refs_1_ = bf16[64,2,128,128]{3,2,1,0:T(8,128)(2,1)} reshape(bf16[64,2,16384]{2,1,0:T(2,128)(2,1)} %param.23) | data formatting | bytes 8388608 | tf_op jit(solution)/shard_map/reshape | solution.py:405
  24.5 44.9 %all-to-all-done.refs_0_ = bf16[16,64,2,8,128]{4,3,2,1,0:T(8,128)(2,1)} async-done(((bf16[16,64,2,8,128]{4,3,2,1,0:T(8,128)(2,1)}), bf16[16,64,2,8,128]{4,3,2,1,0:T(8,128)(2,1)}, u32[]{:S(2)}, u32[]{:S(2)}) %all-to-all-start) | async-done | bytes 4194336 | tf_op jit(solution)/shard_map/all_to_all | solution.py:404
  69.5 23.6 %focus.1.refs_1_ = bf16[16384,128]{1,0:T(8,128)(2,1)} custom-call(bf16[16,64,2,8,128]{4,3,2,1,0:T(8,128)(2,1)} %all-to-all-done.refs_0_, bf16[64,2,128,128]{3,2,1,0:T(8,128)(2,1)} %reshape.90.refs_1_, bf16[256,256]{1,0:T(8,128)(2,1)} %constant.61.clone.refs_2_.refs_4_.refs_3_, bf16[256,256]{1,0:T(8,128)(2,1)} %constant.62.clone.refs_3_.refs_5_, ...), custom_call_target="tpu_custom_call" | custom-call | tf_op jit(solution)/shard_map/focus/pallas_call | solution.py:120
  93.0 11.7 %shard_map.208 = (bf16[16,3,64,128]{3,2,1,0:T(8,128)(2,1)}, bf16[16,3,64,128]{3,2,1,0:T(8,128)(2,1)}) custom-call(s32[512]{0:T(512)} %reshape.91.refs_0_, bf16[16384,128]{1,0:T(8,128)(2,1)} %focus.1.refs_1_, bf16[512,1024]{1,0:T(8,128)(2,1)} %constant.64.clone.refs_2_, bf16[128,256]{1,0:T(8,128)(2,1)} %constant.65.clone.refs_3_), custom_call_target="tpu_custom_call" | custom-call | tf_op jit(solution)/shard_map/pallas_call | solution.py:224
  104.7 1.3 collective-permute-start.3
  106.1 3.3 %collective-permute-start.2 = (bf16[16,3,64,128]{3,2,1,0:T(8,128)(2,1)}, bf16[16,3,64,128]{3,2,1,0:T(8,128)(2,1)S(1)}, u32[]{:S(2)}, u32[]{:S(2)}) collective-permute-start(bf16[16,3,64,128]{3,2,1,0:T(8,128)(2,1)} %get-tuple-element.9.refs_4_), channel_id=1, source_target_pairs={{16,0},{17,1},{18,2},{19,3},{20,4},{21,5},{22,6},{32,16},{33,17},{... | collective-permute-start | bytes 2359304 | tf_op jit(solution)/shard_map/ppermute | solution.py:417
  111.0 13.0 %shard_map.209 = (bf16[16,3,64,128]{3,2,1,0:T(8,128)(2,1)}, bf16[16,3,64,128]{3,2,1,0:T(8,128)(2,1)}) custom-call(s32[512]{0:T(512)} %reshape.91.refs_0_, bf16[16384,128]{1,0:T(8,128)(2,1)} %focus.1.refs_1_, bf16[512,1024]{1,0:T(8,128)(2,1)} %constant.64.clone.refs_2_, bf16[128,256]{1,0:T(8,128)(2,1)} %constant.65.clone.refs_3_, ...), custom_call_target="tpu_custom_call" | custom-call | tf_op jit(solution)/shard_map/pallas_call | solution.py:224
  124.0 6.3 %shard_map.210.refs_4_.refs_1_ = bf16[16,3,128,128]{3,2,1,0:T(8,128)(2,1)} custom-call(s32[512]{0:T(512)} %reshape.88.refs_0_, bf16[16384,128]{1,0:T(8,128)(2,1)} %focus.1.refs_1_, bf16[512,1024]{1,0:T(8,128)(2,1)} %constant.64.clone.refs_2_, bf16[128,256]{1,0:T(8,128)(2,1)} %constant.65.clone.refs_3_, bf16[16,3,64,128]{3,2,1,0:T(8,128)(2,1)} %get-tuple-element.10.refs_4_), custom_call_target="tpu_custom_call" | custom-call | tf_op jit(solution)/shard_map/pallas_call | solution.py:224
  130.3 6.3 %shard_map.211.refs_1_.refs_4_ = bf16[16,3,128,128]{3,2,1,0:T(8,128)(2,1)} custom-call(s32[512]{0:T(512)} %reshape.88.refs_0_, bf16[16384,128]{1,0:T(8,128)(2,1)} %focus.1.refs_1_, bf16[512,1024]{1,0:T(8,128)(2,1)} %constant.64.clone.refs_2_, bf16[128,256]{1,0:T(8,128)(2,1)} %constant.65.clone.refs_3_, bf16[16,3,128,128]{3,2,1,0:T(8,128)(2,1)} %shard_map.210.refs_4_.refs_1_), custom_call_target="tpu_custom_call" | custom-call | tf_op jit(solution)/shard_map/pallas_call | solution.py:224
  137.5 0.9 copy-done.3
  138.4 4.7 %shard_map.213 = bf16[16,3,128,128]{3,2,1,0:T(8,128)(2,1)} custom-call(s32[128]{0:T(128)} %reshape.87.refs_0_, bf16[16,3,128,128]{3,2,1,0:T(8,128)(2,1)} %shard_map.210.refs_4_.refs_1_, bf16[16,3,64,128]{3,2,1,0:T(8,128)(2,1)} %copy-done.3, bf16[16,3,64,128]{3,2,1,0:T(8,128)(2,1)} %copy-done.2, bf16[16,3,128,128]{3,2,1,0:T(8,128)(2,1)} %shard_map.211.refs_1_.refs_4_), custom_call_target="tpu_custom_call" | custom-call | tf_op jit(solution)/shard_map/pallas_call | solution.py:264
  143.1 5.3 %all-to-all-start.2 = ((bf16[16,3,128,128]{3,2,1,0:T(8,128)(2,1)}), bf16[16,3,128,128]{3,2,1,0:T(8,128)(2,1)S(1)}, u32[]{:S(2)}, u32[]{:S(2)}) async-start(bf16[16,3,128,128]{3,2,1,0:T(8,128)(2,1)} %shard_map.213), calls=%async_computation.2 | async-start | bytes 3145728 | tf_op jit(solution)/shard_map/all_to_all | solution.py:426
  148.4 1.3 collective-permute-start.1
  149.8 4.7 %collective-permute-start = (bf16[16,3,64,128]{3,2,1,0:T(8,128)(2,1)S(1)}, bf16[16,3,64,128]{3,2,1,0:T(8,128)(2,1)}, u32[]{:S(2)}, u32[]{:S(2)}) collective-permute-start(bf16[16,3,64,128]{3,2,1,0:T(8,128)(2,1)S(1)} %copy-done.4), channel_id=1, source_target_pairs={{16,0},{17,1},{18,2},{19,3},{20,4},{21,5},{22,6},{32,16},{33,17},{... | collective-permute-start | bytes 2359304 | tf_op jit(solution)/shard_map/ppermute | solution.py:417
  154.5 13.2 %collective-permute-done.1.refs_3_ = bf16[16,3,64,128]{3,2,1,0:T(8,128)(2,1)S(1)} collective-permute-done((bf16[16,3,64,128]{3,2,1,0:T(8,128)(2,1)}, bf16[16,3,64,128]{3,2,1,0:T(8,128)(2,1)S(1)}, u32[]{:S(2)}, u32[]{:S(2)}) %collective-permute-start.1) | collective-permute-done | bytes 786464 | tf_op jit(solution)/shard_map/ppermute | solution.py:417
  167.6 21.2 %collective-permute-done.refs_2_ = bf16[16,3,64,128]{3,2,1,0:T(8,128)(2,1)} collective-permute-done((bf16[16,3,64,128]{3,2,1,0:T(8,128)(2,1)S(1)}, bf16[16,3,64,128]{3,2,1,0:T(8,128)(2,1)}, u32[]{:S(2)}, u32[]{:S(2)}) %collective-permute-start) | collective-permute-done | bytes 786464 | tf_op jit(solution)/shard_map/ppermute | solution.py:417
  188.9 4.7 %shard_map.212 = bf16[16,3,128,128]{3,2,1,0:T(8,128)(2,1)} custom-call(s32[128]{0:T(128)} %reshape.87.refs_0_, bf16[16,3,128,128]{3,2,1,0:T(8,128)(2,1)} %shard_map.211.refs_1_.refs_4_, bf16[16,3,64,128]{3,2,1,0:T(8,128)(2,1)} %collective-permute-done.refs_2_, bf16[16,3,64,128]{3,2,1,0:T(8,128)(2,1)} %copy-done.5, ...), custom_call_target="tpu_custom_call" | custom-call | tf_op jit(solution)/shard_map/pallas_call | solution.py:264
  193.6 4.5 %all-to-all-start.1 = ((bf16[16,3,128,128]{3,2,1,0:T(8,128)(2,1)}), bf16[16,3,128,128]{3,2,1,0:T(8,128)(2,1)S(1)}, u32[]{:S(2)}, u32[]{:S(2)}) async-start(bf16[16,3,128,128]{3,2,1,0:T(8,128)(2,1)} %shard_map.212), calls=%async_computation.1 | async-start | bytes 3145728 | tf_op jit(solution)/shard_map/all_to_all | solution.py:426
  198.9 5.7 %shard_map.214.refs_4_ = f32[4,2,512,128]{3,2,1,0:T(8,128)} custom-call(s32[8]{0:T(128)} %reshape.86.refs_0_, bf16[16,3,128,128]{3,2,1,0:T(8,128)(2,1)} %copy-done, bf16[512,1024]{1,0:T(8,128)(2,1)} %constant.64.clone.refs_2_, bf16[256,256]{1,0:T(8,128)(2,1)} %constant.61.clone.refs_2_.refs_4_.refs_3_), custom_call_target="tpu_custom_call" | custom-call | tf_op jit(solution)/shard_map/pallas_call | solution.py:326
  204.6 15.6 %all-to-all-done.1.refs_1_ = bf16[16,3,128,128]{3,2,1,0:T(8,128)(2,1)S(1)} async-done(((bf16[16,3,128,128]{3,2,1,0:T(8,128)(2,1)}), bf16[16,3,128,128]{3,2,1,0:T(8,128)(2,1)S(1)}, u32[]{:S(2)}, u32[]{:S(2)}) %all-to-all-start.1) | async-done | bytes 1572896 | tf_op jit(solution)/shard_map/all_to_all | solution.py:426
  220.2 1.1 copy-done.1
  221.3 5.7 %shard_map.215 = f32[4,2,512,128]{3,2,1,0:T(8,128)} custom-call(s32[8]{0:T(128)} %reshape.86.refs_0_, bf16[16,3,128,128]{3,2,1,0:T(8,128)(2,1)} %copy-done.1, bf16[512,1024]{1,0:T(8,128)(2,1)} %constant.64.clone.refs_2_, bf16[256,256]{1,0:T(8,128)(2,1)} %constant.61.clone.refs_2_.refs_4_.refs_3_, ...), custom_call_target="tpu_custom_call", output_to_operand_aliasing={{}: (4, {})} | custom-call | tf_op jit(solution)/shard_map/pallas_call | solution.py:326
  (48 shorter events, 6.6 us)
Async XLA Ops:
  7.6 6.4 %copy-start.6 = (s32[8,63]{1,0:T(8,128)S(1)}, s32[8,63]{1,0:T(8,128)}, u32[]{:S(2)}) copy-start(s32[8,63]{1,0:T(8,128)} %param.25) | copy-start | bytes 6052
  7.6 61.9 %all-to-all-start = ((bf16[16,64,2,8,128]{4,3,2,1,0:T(8,128)(2,1)}), bf16[16,64,2,8,128]{4,3,2,1,0:T(8,128)(2,1)}, u32[]{:S(2)}, u32[]{:S(2)}) async-start(bf16[16,64,2,8,128]{4,3,2,1,0:T(8,128)(2,1)} %reshape.89), calls=%async_computation | async-start | bytes 8388608 | tf_op jit(solution)/shard_map/all_to_all | solution.py:404
  104.7 31.9 %collective-permute-start.3 = (bf16[16,3,64,128]{3,2,1,0:T(8,128)(2,1)}, bf16[16,3,64,128]{3,2,1,0:T(8,128)(2,1)S(1)}, u32[]{:S(2)}, u32[]{:S(2)}) collective-permute-start(bf16[16,3,64,128]{3,2,1,0:T(8,128)(2,1)} %get-tuple-element.12), channel_id=1, source_target_pairs={{16,8},{17,9},{18,10},{19,11},{20,12},{21,13},{22,14},{32,24},{33,... | collective-permute-start | bytes 2359304 | tf_op jit(solution)/shard_map/ppermute | solution.py:417
  106.1 30.5 %collective-permute-start.2 = (bf16[16,3,64,128]{3,2,1,0:T(8,128)(2,1)}, bf16[16,3,64,128]{3,2,1,0:T(8,128)(2,1)S(1)}, u32[]{:S(2)}, u32[]{:S(2)}) collective-permute-start(bf16[16,3,64,128]{3,2,1,0:T(8,128)(2,1)} %get-tuple-element.9.refs_4_), channel_id=1, source_target_pairs={{16,0},{17,1},{18,2},{19,3},{20,4},{21,5},{22,6},{32,16},{33,17},{... | collective-permute-start | bytes 2359304 | tf_op jit(solution)/shard_map/ppermute | solution.py:417
  136.6 0.9 copy-start.2
  137.5 0.9 copy-start.3
  143.1 6.7 %copy-start.4 = (bf16[16,3,64,128]{3,2,1,0:T(8,128)(2,1)S(1)}, bf16[16,3,64,128]{3,2,1,0:T(8,128)(2,1)}, u32[]{:S(2)}) copy-start(bf16[16,3,64,128]{3,2,1,0:T(8,128)(2,1)} %get-tuple-element.10.refs_4_) | copy-start | bytes 2359300
  143.1 50.5 %all-to-all-start.2 = ((bf16[16,3,128,128]{3,2,1,0:T(8,128)(2,1)}), bf16[16,3,128,128]{3,2,1,0:T(8,128)(2,1)S(1)}, u32[]{:S(2)}, u32[]{:S(2)}) async-start(bf16[16,3,128,128]{3,2,1,0:T(8,128)(2,1)} %shard_map.213), calls=%async_computation.2 | async-start | bytes 3145728 | tf_op jit(solution)/shard_map/all_to_all | solution.py:426
  148.4 19.2 %collective-permute-start.1 = (bf16[16,3,64,128]{3,2,1,0:T(8,128)(2,1)}, bf16[16,3,64,128]{3,2,1,0:T(8,128)(2,1)S(1)}, u32[]{:S(2)}, u32[]{:S(2)}) collective-permute-start(bf16[16,3,64,128]{3,2,1,0:T(8,128)(2,1)} %get-tuple-element.11), channel_id=1, source_target_pairs={{16,8},{17,9},{18,10},{19,11},{20,12},{21,13},{22,14},{32,24},{33,... | collective-permute-start | bytes 2359304 | tf_op jit(solution)/shard_map/ppermute | solution.py:417
  149.8 39.1 %collective-permute-start = (bf16[16,3,64,128]{3,2,1,0:T(8,128)(2,1)S(1)}, bf16[16,3,64,128]{3,2,1,0:T(8,128)(2,1)}, u32[]{:S(2)}, u32[]{:S(2)}) collective-permute-start(bf16[16,3,64,128]{3,2,1,0:T(8,128)(2,1)S(1)} %copy-done.4), channel_id=1, source_target_pairs={{16,0},{17,1},{18,2},{19,3},{20,4},{21,5},{22,6},{32,16},{33,17},{... | collective-permute-start | bytes 2359304 | tf_op jit(solution)/shard_map/ppermute | solution.py:417
  167.6 21.3 %copy-start.5 = (bf16[16,3,64,128]{3,2,1,0:T(8,128)(2,1)}, bf16[16,3,64,128]{3,2,1,0:T(8,128)(2,1)S(1)}, u32[]{:S(2)}) copy-start(bf16[16,3,64,128]{3,2,1,0:T(8,128)(2,1)S(1)} %collective-permute-done.1.refs_3_) | copy-start | bytes 2359300
  193.6 5.3 %copy-start = (bf16[16,3,128,128]{3,2,1,0:T(8,128)(2,1)}, bf16[16,3,128,128]{3,2,1,0:T(8,128)(2,1)S(1)}, u32[]{:S(2)}) copy-start(bf16[16,3,128,128]{3,2,1,0:T(8,128)(2,1)S(1)} %all-to-all-done.2.refs_1_) | copy-start | bytes 4718596
  193.6 26.6 %all-to-all-start.1 = ((bf16[16,3,128,128]{3,2,1,0:T(8,128)(2,1)}), bf16[16,3,128,128]{3,2,1,0:T(8,128)(2,1)S(1)}, u32[]{:S(2)}, u32[]{:S(2)}) async-start(bf16[16,3,128,128]{3,2,1,0:T(8,128)(2,1)} %shard_map.212), calls=%async_computation.1 | async-start | bytes 3145728 | tf_op jit(solution)/shard_map/all_to_all | solution.py:426
  220.2 1.2 copy-start.1
